TPU v7x, 128 devices: a whole 4x4x4 slice. The times are simulated.
128 devices in a mesh: req: 8 (over y, core), hid: 16 (over x, z).
Axes of the slice: x: 4, y: 4, z: 4, core: 2. Of those that a mesh axis runs over, the one named last changes fastest.
Arguments:
- merged: bfloat16 [8, 256, 12800], P(None, 'req', 'hid')
- ln_gain: bfloat16 [12800], replicated, may hold values from 0.25 to 1.75
- ln_bias: bfloat16 [12800], replicated, may hold values from -3 to 3
- proj_weight: bfloat16 [12800, 6144], P(None, 'hid'), may hold values from -0.0546875 to 0.0546875
- proj_bias: float32 [6144], P('hid'), may hold values from -3 to 3
- text_embed: bfloat16 [16, 480, 6144], P('req', None, 'hid')
- attn_gain: bfloat16 [6144], replicated, may hold values from 0.25 to 1.75
- query_weight: bfloat16 [6144, 6144], P(None, 'hid')
- key_weight: bfloat16 [6144, 1024], P(None, 'hid')
- value_weight: bfloat16 [6144, 1024], P(None, 'hid'), may hold values from -0.078125 to 0.078125
- out_weight: bfloat16 [6144, 6144], P('hid'), may hold values from -0.078125 to 0.078125
- final_gain: bfloat16 [6144], replicated, may hold values from 0.25 to 1.75
- head_weight: bfloat16 [49152, 6144], P(('req', 'hid')), may hold values from -0.23925781 to 0.23925781
- lengths: int32 [16], P('req'), may hold values from 160 to 480, as said below
- tile_request: int32 [8], replicated, may hold values from 0 to 15, as said below
- insert_pos: int32 [8], replicated, may hold values from 0 to 224, as said below
Outputs:
- hidden: bfloat16 [16, 480, 6144], P('req', None, 'hid')
- final_norm: float32 [16], replicated
- logit_max: float32 [16], replicated
Inputs may be any that keep to these rules, and one draw needn't show every extreme that they name: For every g, the requests 2g and 2g + 1 have lengths that add up to exactly 640. `tile_request`: each pair of requests 2g, 2g + 1 holds exactly one tile, in the one of the two whose length is not smaller. insert_pos[t] + 256 is at most the length of request tile_request[t].
All inputs are finite; a program needn't handle non-finite values.
Results may differ from a plain program's by a relative error of at most 0.0095.
Values may be sent and summed in bfloat16 or wider, within the bound.
No kernel may reach another device: no remote copies, remote signals or barrier semaphores. Data moves between devices by JAX's collectives and lax.ppermute only.
A program may use at most 128 MiB of HBM per device.

v0:
```python
import math
import jax
import jax.numpy as jnp
from jax import lax
from jax.sharding import PartitionSpec as P

HEAD_DIM = 128
D = 6144
REQ_GRP = 2


def from_partner(block, axis, stride):
    count = lax.axis_size(axis)
    route = []
    for low in range(count):
        high = low | 1 << stride
        if high != low and high < count:
            route += [(low, high), (high, low)]
    return lax.ppermute(block, axis, route)


def rotary(values, positions):
    half_dim = values.shape[-1] // 2
    inv_freq = jnp.exp(
        jnp.arange(half_dim, dtype=jnp.float32) * (-2.0 * math.log(1000000.0) / values.shape[-1])
    )
    angles = positions.astype(jnp.float32)[:, None] * inv_freq[None, :]
    cosine = jnp.cos(angles)[:, None, :]
    sine_val = jnp.sin(angles)[:, None, :]
    first_half = values[..., :half_dim]
    second = values[..., half_dim:]
    return jnp.concatenate(
        [first_half * cosine - second * sine_val, second * cosine + first_half * sine_val], axis=-1
    )


def attend_local(queries, key_rows, value_rows, length):
    scores = jnp.einsum(
        "qhd,sd->hqs", queries, key_rows, preferred_element_type=jnp.float32
    ) / math.sqrt(HEAD_DIM)
    positions = jnp.arange(queries.shape[0])
    allowed = positions[None, :] <= positions[:, None]
    scores = jnp.where(allowed[None], scores, -jnp.inf)
    row_top = jnp.max(scores, axis=-1, keepdims=True)
    weights = jnp.exp(scores - row_top)
    weights = (weights / jnp.sum(weights, axis=-1, keepdims=True)).astype(jnp.bfloat16)
    mixed_out = jnp.einsum("hqs,sd->qhd", weights, value_rows, preferred_element_type=jnp.float32)
    mixed_out = jnp.where((positions < length)[:, None, None], mixed_out, 0.0)
    return mixed_out.reshape(queries.shape[0], -1).astype(jnp.bfloat16)


def shards(
    merged,
    ln_gain,
    ln_bias,
    proj_weight,
    proj_bias,
    text_embed,
    attn_gain,
    query_weight,
    key_weight,
    value_weight,
    out_weight,
    final_gain,
    head_weight,
    lengths,
    tile_request,
    insert_pos,
):
    owners = tile_request // REQ_GRP
    tile_order = jnp.argsort(owners)
    outgoing = merged[tile_order]
    arrived = lax.all_to_all(outgoing, "req", split_axis=0, concat_axis=1, tiled=True)
    features = lax.all_gather(arrived[0], "hid", axis=1, tiled=True)
    values = features.astype(jnp.float32)
    row_mean = jnp.mean(values, axis=1, keepdims=True)
    row_var = jnp.mean(values * values, axis=1, keepdims=True) - row_mean * row_mean
    normed = (
        (values - row_mean) * lax.rsqrt(row_var + 1e-05) * ln_gain.astype(jnp.float32)
        + ln_bias.astype(jnp.float32)
    ).astype(jnp.bfloat16)
    projected = jnp.dot(normed, proj_weight, preferred_element_type=jnp.float32) + proj_bias
    projected = jax.nn.gelu(projected, approximate=False).astype(jnp.bfloat16)
    own_tile = tile_order[lax.axis_index("req")]
    local_req = tile_request[own_tile] % REQ_GRP
    embedded = lax.dynamic_update_slice(
        text_embed, projected[None], (local_req, insert_pos[own_tile], jnp.zeros((), jnp.int32))
    )
    length_max = text_embed.shape[1]
    flat_rows = embedded.reshape(REQ_GRP * length_max, -1)
    position = jnp.arange(length_max)
    gain_part = attn_gain.astype(jnp.float32)
    portion_f = lax.all_gather(flat_rows, "hid", axis=1, tiled=True).astype(jnp.float32)
    scaled = (portion_f * gain_part).astype(jnp.bfloat16)
    squares = jnp.sum(portion_f * portion_f, axis=1)
    q_total = jnp.dot(scaled, query_weight, preferred_element_type=jnp.float32)
    k_total = jnp.dot(scaled, key_weight, preferred_element_type=jnp.float32)
    v_total = jnp.dot(scaled, value_weight, preferred_element_type=jnp.float32)
    row_scale = lax.rsqrt(squares / D + 1e-05)[:, None]
    queries = q_total * row_scale
    key_half = (k_total * row_scale).astype(jnp.bfloat16)
    value_half = (v_total * row_scale).astype(jnp.bfloat16)
    other_key, other_value = from_partner((key_half, value_half), "hid", 0)
    is_lower = lax.axis_index("hid") % 2 == 0
    key_raw = jnp.where(
        is_lower,
        jnp.concatenate([key_half, other_key], 1),
        jnp.concatenate([other_key, key_half], 1),
    )
    kv_values = jnp.where(
        is_lower,
        jnp.concatenate([value_half, other_value], 1),
        jnp.concatenate([other_value, value_half], 1),
    )
    heads_local = queries.shape[1] // HEAD_DIM
    queries = queries.reshape(REQ_GRP, length_max, heads_local, HEAD_DIM)
    key_raw = key_raw.reshape(REQ_GRP, length_max, 1, HEAD_DIM)
    kv_values = kv_values.reshape(REQ_GRP, length_max, HEAD_DIM)
    pieces = []
    for request in range(REQ_GRP):
        q_rotated = rotary(queries[request], position).astype(jnp.bfloat16)
        k_rotated = rotary(key_raw[request].astype(jnp.float32), position).astype(jnp.bfloat16)[
            :, 0, :
        ]
        pieces.append(attend_local(q_rotated, k_rotated, kv_values[request], lengths[request]))
    attended = jnp.concatenate(pieces, axis=0)
    partial_value = jnp.dot(attended, out_weight, preferred_element_type=jnp.float32)
    attn_sum = lax.psum_scatter(
        partial_value.astype(jnp.bfloat16), "hid", scatter_dimension=1, tiled=True
    ).astype(jnp.float32)
    hidden = (
        (flat_rows.astype(jnp.float32) + attn_sum)
        .astype(jnp.bfloat16)
        .reshape(REQ_GRP, length_max, -1)
    )
    last_rows = hidden[jnp.arange(REQ_GRP), lengths - 1]
    full_width = lax.all_gather(last_rows, "hid", axis=1, tiled=True)
    all_last = lax.all_gather(full_width, "req", axis=0, tiled=True)
    last_values = all_last.astype(jnp.float32)
    last_squares = jnp.sum(last_values * last_values, axis=1)
    final_norm = jnp.sqrt(last_squares)
    final_scaled = (
        last_values * lax.rsqrt(last_squares / D + 1e-05)[:, None] * final_gain.astype(jnp.float32)
    ).astype(jnp.bfloat16)
    logits = lax.dot_general(
        final_scaled, head_weight, (((1,), (1,)), ((), ())), preferred_element_type=jnp.float32
    )
    logit_max = lax.pmax(jnp.max(logits, axis=1), ("req", "hid"))
    return (hidden, final_norm, logit_max)


def solution(mesh):
    return jax.shard_map(
        shards,
        mesh=mesh,
        in_specs=(
            P(None, "req", "hid"),
            P(),
            P(),
            P(None, "hid"),
            P("hid"),
            P("req", None, "hid"),
            P(),
            P(None, "hid"),
            P(None, "hid"),
            P(None, "hid"),
            P("hid", None),
            P(),
            P(("req", "hid"), None),
            P("req"),
            P(),
            P(),
        ),
        out_specs=(P("req", None, "hid"), P(), P()),
        check_vma=False,
    )
```

profile of v0, /device:TPU:1, one launch (start us, length us, event | category | flops | bytes accessed | tf_op | source)
XLA Modules:
  0.0 486.7 jit_solution(6029854030120784377)
XLA Ops:
  8.9 1.6 gather_fusion
  10.6 14.5 %all_to_all.4 = bf16[8,32,800]{2,1,0:T(8,128)(2,1)S(1)} all-to-all(bf16[8,32,800]{2,1,0:T(8,128)(2,1)S(1)} %gather_fusion), channel_id=1, replica_groups=mesh['req'=8,'hid'=16] {'req'}, dimensions={0} | all-to-all | bytes 819200 | tf_op jit(solution)/shard_map/all_to_all | solution.py:73
  31.9 1.2 dynamic_slice.11
  35.8 53.5 %all-gather.4.cloned.1.call-done = bf16[256,12800]{0,1:T(8,128)(2,1)} async-done(((bf16[256,800]{0,1:T(8,128)(2,1)}), bf16[256,12800]{0,1:T(8,128)(2,1)}) %all-gather.4.cloned.1.call-update) | async-done | bytes 6553616 | tf_op jit(solution)/shard_map/all_gather | solution.py:74
  89.4 4.9 %convert_reduce_fusion = (f32[256]{0:T(256)S(1)}, f32[256]{0:T(256)S(1)}) fusion(bf16[256,12800]{0,1:T(8,128)(2,1)} %all-gather.4.cloned.1.call-done), kind=kLoop, calls=%fused_computation.10 | loop fusion | flops 13106688 | bytes 6555648 | tf_op jit(solution)/shard_map/reduce_sum | solution.py:76
  94.3 15.5 %fusion.70 = bf16[1,256,384]{2,1,0:T(8,128)(2,1)S(1)} fusion(bf16[12800,384]{1,0:T(8,128)(2,1)} %param.19, bf16[256,12800]{0,1:T(8,128)(2,1)S(1)} %copy-done.6, f32[12800]{0:T(1024)S(1)} %convert_element_type.139, f32[12800]{0:T(1024)S(1)} %convert_element_type.138, f32[256]{0:T(256)S(1)} %get-tuple-element.30, f32[256]{0:T(256)S(1)} %get-tuple-element.29, ...), kind=kOutput, calls=%fused_computation.84 | convolution fusion | flops 2542731264 | bytes 16686592 | tf_op jit(solution)/shard_map/dot_general | solution.py:82
  109.9 1.4 dynamic_update_slice.3
  113.0 1.2 iota_compare_fusion.2
  116.2 1.7 multiply_cosine_fusion
  117.9 88.9 %all-gather.6.cloned.1.call-done = bf16[960,6144]{1,0:T(8,128)(2,1)} async-done(((bf16[960,384]{1,0:T(8,128)(2,1)}), bf16[960,6144]{1,0:T(8,128)(2,1)}) %all-gather.6.cloned.1.call-update) | async-done | bytes 11796496 | tf_op jit(solution)/shard_map/all_gather | solution.py:93
  206.8 6.8 %fusion.3 = f32[960]{0:T(1024)S(1)} fusion(bf16[960,6144]{1,0:T(8,128)(2,1)} %all-gather.6.cloned.1.call-done), kind=kLoop, calls=%fused_computation.7 | loop fusion | flops 17693760 | bytes 11800320 | tf_op jit(solution)/shard_map/reduce_sum | solution.py:95
  213.6 8.1 %fusion.52 = bf16[960,64]{0,1:T(8,128)(2,1)S(1)} fusion(bf16[6144,64]{0,1:T(8,128)(2,1)S(1)} %copy-done, bf16[960,6144]{1,0:T(8,128)(2,1)} %all-gather.6.cloned.1.call-done, f32[6144]{0:T(1024)S(1)} %convert_element_type.144, f32[960]{0:T(1024)S(1)} %add_rsqrt_fusion), kind=kOutput, calls=%fused_computation.53 | convolution fusion | flops 772792320 | bytes 12734208 | tf_op jit(solution)/shard_map/dot_general | solution.py:97
  222.9 6.3 %fusion.23 = f32[960,384]{1,0:T(8,128)S(1)} fusion(bf16[6144,384]{1,0:T(8,128)(2,1)S(1)} %bitcast.98, bf16[960,6144]{1,0:T(8,128)(2,1)S(1)} %copy-done.2, f32[6144]{0:T(1024)S(1)} %convert_element_type.144, f32[960]{0:T(1024)S(1)} %add_rsqrt_fusion), kind=kOutput, calls=%fused_computation.33 | convolution fusion | flops 4547911680 | bytes 18018048 | tf_op jit(solution)/shard_map/dot_general | solution.py:96
  231.1 8.2 %fusion.46 = bf16[960,64]{0,1:T(8,128)(2,1)S(1)} fusion(bf16[6144,64]{0,1:T(8,128)(2,1)} %param.25, bf16[960,6144]{1,0:T(8,128)(2,1)} %all-gather.6.cloned.1.call-done, f32[6144]{0:T(1024)S(1)} %convert_element_type.144, f32[960]{0:T(1024)S(1)} %add_rsqrt_fusion), kind=kOutput, calls=%fused_computation.51 | convolution fusion | flops 772792320 | bytes 12734208 | tf_op jit(solution)/shard_map/dot_general | solution.py:98
  243.7 1.5 fusion.123
  247.0 1.5 fusion.122
  249.6 12.0 %convolution_convert_fusion = bf16[960,6144]{1,0:T(8,128)(2,1)} fusion(bf16[384,6144]{1,0:T(8,128)(2,1)} %param.26, bf16[480,384]{0,1:T(8,128)(2,1)S(1)} %bitcast.92, bf16[480,384]{0,1:T(8,128)(2,1)S(1)} %bitcast.91), kind=kOutput, calls=%fused_computation.16 | convolution fusion | flops 4537221120 | bytes 17252352 | tf_op jit(solution)/shard_map/dot_general | solution.py:127
  261.6 16.4 %copy.83 = bf16[960,6144]{0,1:T(8,128)(2,1)} copy(bf16[960,6144]{1,0:T(8,128)(2,1)} %convolution_convert_fusion) | data formatting | bytes 23592960
  278.8 94.4 %reduce-scatter.4.cloned.1.call-done = bf16[384,960]{1,0:T(8,128)(2,1)} async-done(((bf16[6144,960]{1,0:T(8,128)(2,1)}), bf16[384,960]{1,0:T(8,128)(2,1)}) %reduce-scatter.4.cloned.1.call-update) | async-done | bytes 737296
  373.2 1.6 copy.84
  375.7 15.8 %all_gather.14 = bf16[2,6144]{1,0:T(2,128)(2,1)S(1)} all-gather(bf16[2,384]{1,0:T(2,128)(2,1)S(1)} %gather_fusion.1), channel_id=1, replica_groups=mesh['req'=8,'hid'=16] {'hid'}, dimensions={1}, use_global_device_ids=true | all-gather | bytes 26112 | tf_op jit(solution)/shard_map/all_gather | solution.py:137
  391.5 20.4 %all-gather = bf16[8,2,6144]{2,1,0:T(2,128)(2,1)S(1)} all-gather(bf16[1,2,6144]{2,1,0:T(2,128)(2,1)S(1)} %bitcast.96), channel_id=1, replica_groups=mesh['req'=8,'hid'=16] {'req'}, dimensions={0}, use_global_device_ids=true | all-gather | bytes 221184 | tf_op jit(solution)/shard_map/all_gather | solution.py:138
  412.6 3.8 convolution_reduce_fusion
  416.4 63.8 %pmax.7 = f32[16]{0:T(128)} all-reduce(f32[16]{0:T(128)S(1)} %convolution_reduce_fusion), channel_id=1, replica_groups=mesh['req'=8,'hid'=16] {'req','hid'}, use_global_device_ids=true, to_apply=%region_11.12 | all-reduce | flops 16 | bytes 128 | tf_op jit(solution)/shard_map/pmax | solution.py:148
  (106 shorter events, 21.3 us)
Async XLA Ops:
  7.2 206.4 %copy-start = (bf16[6144,64]{0,1:T(8,128)(2,1)S(1)}, bf16[6144,64]{0,1:T(8,128)(2,1)}, u32[]{:S(2)}) copy-start(bf16[6144,64]{0,1:T(8,128)(2,1)} %param.24) | copy-start | bytes 2359300
  7.2 28.0 %copy-start.13 = (bf16[12800]{0:T(1024)(128)(2,1)S(1)}, bf16[12800]{0:T(1024)(128)(2,1)}, u32[]{:S(2)}) copy-start(bf16[12800]{0:T(1024)(128)(2,1)} %param.18) | copy-start | bytes 76804
  7.2 82.2 %all-gather.4.cloned.1.call-start = ((), (), s32[]{:S(2)}) async-start(), calls=%async_computation.2 | async-start | bytes 6963200 | tf_op jit(solution)/shard_map/all_gather | solution.py:74
  10.6 83.7 %copy-start.20 = (f32[384]{0:T(512)S(1)}, f32[384]{0:T(512)}, u32[]{:S(2)}) copy-start(f32[384]{0:T(512)} %param.20) | copy-start | bytes 4612
  26.1 180.7 %all-gather.6.cloned.1.call-start = ((), (), s32[]{:S(2)}) async-start(), calls=%async_computation.3 | async-start | bytes 12533760 | tf_op jit(solution)/shard_map/all_gather | solution.py:93
  89.4 4.9 %copy-start.6 = (bf16[256,12800]{0,1:T(8,128)(2,1)S(1)}, bf16[256,12800]{0,1:T(8,128)(2,1)}, u32[]{:S(2)}) copy-start(bf16[256,12800]{0,1:T(8,128)(2,1)} %all-gather.4.cloned.1.call-done) | copy-start | bytes 19660804
  94.3 15.6 %copy-start.5 = (bf16[2,480,384]{2,1,0:T(8,128)(2,1)S(1)}, bf16[2,480,384]{2,1,0:T(8,128)(2,1)}, u32[]{:S(2)}) copy-start(bf16[2,480,384]{2,1,0:T(8,128)(2,1)} %param.21) | copy-start | bytes 2211844
  94.3 18.0 %copy-start.14 = (bf16[6144]{0:T(1024)(128)(2,1)S(1)}, bf16[6144]{0:T(1024)(128)(2,1)}, u32[]{:S(2)}) copy-start(bf16[6144]{0:T(1024)(128)(2,1)} %param.22) | copy-start | bytes 36868
  94.3 18.0 %copy-start.16 = (s32[2]{0:T(128)S(1)}, s32[2]{0:T(128)}, u32[]{:S(2)}) copy-start(s32[2]{0:T(128)} %param.29) | copy-start | bytes 28
  112.2 260.9 %reduce-scatter.4.cloned.1.call-start = ((), (), s32[]{:S(2)}) async-start(), calls=%async_computation.4 | async-start | bytes 13369344
  112.3 101.2 %copy-start.18 = (f32[64]{0:T(128)}, f32[64]{0:T(128)S(1)}, u32[]{:S(2)}) copy-start(f32[64]{0:T(128)S(1)} %multiply_exponential_fusion) | copy-start | bytes 772
  206.8 16.1 %slice-start = ((s8[4718592]{0:T(1024)(128)(4,1)}), s8[524288]{0:T(1024)(128)(4,1)S(1)}, s32[]{:S(2)}) async-start(s8[4718592]{0:T(1024)(128)(4,1)} %bitcast.97), calls=%async_computation.5 | async-start | bytes 1048576
  213.6 9.3 %copy-start.2 = (bf16[960,6144]{1,0:T(8,128)(2,1)S(1)}, bf16[960,6144]{1,0:T(8,128)(2,1)}, u32[]{:S(2)}) copy-start(bf16[960,6144]{1,0:T(8,128)(2,1)} %all-gather.6.cloned.1.call-done) | copy-start | bytes 35389444
  213.6 9.3 %slice-start.1 = ((s8[4718592]{0:T(1024)(128)(4,1)}), s8[4194304]{0:T(1024)(128)(4,1)S(1)}, s32[]{:S(2)}) async-start(s8[4718592]{0:T(1024)(128)(4,1)} %bitcast.97), calls=%async_computation.6 | async-start | bytes 8388608
  221.8 19.5 %collective-permute-start.1 = (bf16[960,64]{0,1:T(8,128)(2,1)S(1)}, bf16[960,64]{0,1:T(8,128)(2,1)}, u32[]{:S(2)}, u32[]{:S(2)}) collective-permute-start(bf16[960,64]{0,1:T(8,128)(2,1)S(1)} %fusion.52), channel_id=1, source_target_pairs={{0,1},{1,0},{2,3},{3,2},{4,5},{5,4},{6,7},{7,6},{8,9},{9,8},{10,11... | collective-permute-start | bytes 368648 | tf_op jit(solution)/shard_map/ppermute | solution.py:19
  231.0 9.1 %copy-start.8 = (f32[480,64]{1,0:T(8,128)S(1)}, f32[480,64]{1,0:T(8,128)}, u32[]{:S(2)}) copy-start(f32[480,64]{1,0:T(8,128)} %get-tuple-element.27) | copy-start | bytes 368644
  231.0 9.1 %copy-start.9 = (f32[480,64]{1,0:T(8,128)S(1)}, f32[480,64]{1,0:T(8,128)}, u32[]{:S(2)}) copy-start(f32[480,64]{1,0:T(8,128)} %get-tuple-element.28) | copy-start | bytes 368644
  239.2 3.2 copy-start.19
  239.2 6.0 %collective-permute-start = (bf16[960,64]{0,1:T(8,128)(2,1)S(1)}, bf16[960,64]{0,1:T(8,128)(2,1)S(1)}, u32[]{:S(2)}, u32[]{:S(2)}) collective-permute-start(bf16[960,64]{0,1:T(8,128)(2,1)S(1)} %fusion.46), channel_id=1, source_target_pairs={{0,1},{1,0},{2,3},{3,2},{4,5},{5,4},{6,7},{7,6},{8,9},{9,8},{10,11... | collective-permute-start | bytes 368648 | tf_op jit(solution)/shard_map/ppermute | solution.py:19
  240.1 3.5 copy-start.11
  246.3 2.2 copy-start.21
  278.1 96.7 %copy-start.4 = (bf16[2,480,384]{2,1,0:T(8,128)(2,1)S(1)}, bf16[2,480,384]{2,1,0:T(8,128)(2,1)}, u32[]{:S(2)}) copy-start(bf16[2,480,384]{2,1,0:T(8,128)(2,1)} %copy-done.3) | copy-start | bytes 2211844
  373.2 107.0 %copy-start.1 = (bf16[6144,64]{0,1:T(8,128)(2,1)S(1)}, bf16[6144,64]{0,1:T(8,128)(2,1)}, u32[]{:S(2)}) copy-start(bf16[6144,64]{0,1:T(8,128)(2,1)} %param.24) | copy-start | bytes 2359300
  375.0 105.1 %copy-start.10 = (bf16[960,384]{1,0:T(8,128)(2,1)}, bf16[960,384]{1,0:T(8,128)(2,1)S(1)}, u32[]{:S(2)}) copy-start(bf16[960,384]{1,0:T(8,128)(2,1)S(1)} %add_convert_fusion) | copy-start | bytes 2211844
  (6 other events, 6.6 us)
Sparse Core Ops, SparseCore 0:
  26.2 63.1 all-gather.3
  112.3 94.4 all-gather.5
  278.2 94.9 reduce-scatter.3
where the time goes:
time: 488 us; the launch traced here: 487 us
  waiting for transfers between devices  237 us (49%)
  blocking collectives  114 us (23%)
  matrix products  56.8 us (12%)
  local copies, waits for them, and re-layouts  30.2 us (6%)
  other arithmetic  26 us (5%)
  between operations  20.1 us (4%)
    unnamed x4, waiting for transfers between devices  94.4 us
    all_gather x1, waiting for transfers between devices, shards(): lax.all_gather(flat_rows, 'hid', axis=1, tiled=True).astype(jnp.float32)  88.9 us
    pmax x1, blocking collectives, shards(): logit_max = lax.pmax(jnp.max(logits, axis=1), ('req', 'hid'))  63.8 us
    all_gather x1, waiting for transfers between devices, shards(): features = lax.all_gather(arrived[0], 'hid', axis=1, tiled=True)  53.5 us
    unnamed x56, local copies, waits for them, and re-layouts  20.7 us
    all_gather x1, blocking collectives, shards(): all_last = lax.all_gather(full_width, 'req', axis=0, tiled=True)  20.4 us
    all_gather x1, blocking collectives, shards(): full_width = lax.all_gather(last_rows, 'hid', axis=1, tiled=True)  15.8 us
    dot_general x1, matrix products, shards(): jnp.dot(normed, proj_weight, preferred_element_type=jnp.float32) + proj_bias  15.5 us
  transfers between devices with their start and end apart: 5, of which 3 were waited for; matrix products, arithmetic and copies ran while one was open for 6% of the time, Pallas kernels for 0%

commit v1 on v0

--- a/solution.py
+++ b/solution.py
@@ -135,7 +135,12 @@
     )
     last_rows = hidden[jnp.arange(REQ_GRP), lengths - 1]
     full_width = lax.all_gather(last_rows, "hid", axis=1, tiled=True)
-    all_last = lax.all_gather(full_width, "req", axis=0, tiled=True)
+    ring = [full_width]
+    for hop in range(7):
+        ring.append(lax.ppermute(ring[-1], "req", [(dev, (dev + 1) % 8) for dev in range(8)]))
+    all_last = jnp.roll(
+        jnp.concatenate(ring[::-1], axis=0), (lax.axis_index("req") + 1) * ring[0].shape[0], axis=0
+    )
     last_values = all_last.astype(jnp.float32)
     last_squares = jnp.sum(last_values * last_values, axis=1)
     final_norm = jnp.sqrt(last_squares)

time: 488 us -> 505 us (1.035)
  waiting for transfers between devices: 237 us -> 258 us
  blocking collectives: 114 us -> 95.8 us
  starting transfers between devices: 2.14 us -> 16.6 us
    ppermute x0 -> x7, waiting for transfers between devices: none -> 20.5 us  [shards(): lax.ppermute(ring[-1], 'req', [(dev, (dev + 1) % 8) for dev in range(8)])]
    all_gather x1 -> x0, blocking collectives: 20.4 us -> none  [shards(): all_last = lax.all_gather(full_width, 'req', axis=0, tiled=True)]
    ppermute x0 -> x7, starting transfers between devices: none -> 14.4 us  [shards(): lax.ppermute(ring[-1], 'req', [(dev, (dev + 1) % 8) for dev in range(8)])]
  transfers between devices with their start and end apart: 5 -> 12, of which waited for: 3 -> 10; matrix products, arithmetic and copies ran while one was open for 6% -> 6% of each run, Pallas kernels for 0% -> 0%
where the time goes in v1:
time: 505 us; the launch traced here: 504 us
  waiting for transfers between devices  258 us (51%)
  blocking collectives  95.8 us (19%)
  matrix products  56.8 us (11%)
  local copies, waits for them, and re-layouts  30.7 us (6%)
  other arithmetic  26 us (5%)
  between operations  20.2 us (4%)
  starting transfers between devices  16.6 us (3%)
    unnamed x4, waiting for transfers between devices  94.9 us
    all_gather x1, waiting for transfers between devices, shards(): lax.all_gather(flat_rows, 'hid', axis=1, tiled=True).astype(jnp.float32)  88.9 us
    pmax x1, blocking collectives, shards(): logit_max = lax.pmax(jnp.max(logits, axis=1), ('req', 'hid'))  65.5 us
    all_gather x1, waiting for transfers between devices, shards(): features = lax.all_gather(arrived[0], 'hid', axis=1, tiled=True)  53.5 us
    unnamed x56, local copies, waits for them, and re-layouts  20.6 us
    ppermute x7, waiting for transfers between devices, shards(): lax.ppermute(ring[-1], 'req', [(dev, (dev + 1) % 8) for dev in range(8)])  20.5 us
    all_gather x1, blocking collectives, shards(): full_width = lax.all_gather(last_rows, 'hid', axis=1, tiled=True)  15.8 us
    dot_general x1, matrix products, shards(): jnp.dot(normed, proj_weight, preferred_element_type=jnp.float32) + proj_bias  15.5 us
  transfers between devices with their start and end apart: 12, of which 10 were waited for; matrix products, arithmetic and copies ran while one was open for 6% of the time, Pallas kernels for 0%

profile of v1, /device:TPU:1, one launch (start us, length us, event | category | flops | bytes accessed | tf_op | source)
XLA Modules:
  0.0 503.9 jit_solution(2974722237319108766)
XLA Ops:
  10.6 14.5 %all_to_all.4 = bf16[8,32,800]{2,1,0:T(8,128)(2,1)S(1)} all-to-all(bf16[8,32,800]{2,1,0:T(8,128)(2,1)S(1)} %gather_fusion), channel_id=1, replica_groups=mesh['req'=8,'hid'=16] {'req'}, dimensions={0} | all-to-all | bytes 819200 | tf_op jit(solution)/shard_map/all_to_all | solution.py:73
  35.8 53.5 %all-gather.3.cloned.1.call-done = bf16[256,12800]{0,1:T(8,128)(2,1)} async-done(((bf16[256,800]{0,1:T(8,128)(2,1)}), bf16[256,12800]{0,1:T(8,128)(2,1)}) %all-gather.3.cloned.1.call-update) | async-done | bytes 6553616 | tf_op jit(solution)/shard_map/all_gather | solution.py:74
  89.4 4.9 convert_reduce_fusion
  94.3 15.5 %fusion.73 = bf16[1,256,384]{2,1,0:T(8,128)(2,1)S(1)} fusion(bf16[12800,384]{1,0:T(8,128)(2,1)} %param.19, bf16[256,12800]{0,1:T(8,128)(2,1)S(1)} %copy-done.6, f32[12800]{0:T(1024)S(1)} %convert_element_type.139, f32[12800]{0:T(1024)S(1)} %convert_element_type.138, f32[256]{0:T(256)S(1)} %get-tuple-element.30, f32[256]{0:T(256)S(1)} %get-tuple-element.29, ...), kind=kOutput, calls=%fused_computation.87 | convolution fusion | flops 2542731264 | bytes 16686592 | tf_op jit(solution)/shard_map/dot_general | solution.py:82
  116.2 1.7 multiply_cosine_fusion
  117.9 88.9 %all-gather.5.cloned.1.call-done = bf16[960,6144]{1,0:T(8,128)(2,1)} async-done(((bf16[960,384]{1,0:T(8,128)(2,1)}), bf16[960,6144]{1,0:T(8,128)(2,1)}) %all-gather.5.cloned.1.call-update) | async-done | bytes 11796496 | tf_op jit(solution)/shard_map/all_gather | solution.py:93
  206.8 6.8 %fusion.3 = f32[960]{0:T(1024)S(1)} fusion(bf16[960,6144]{1,0:T(8,128)(2,1)} %all-gather.5.cloned.1.call-done), kind=kLoop, calls=%fused_computation.7 | loop fusion | flops 17693760 | bytes 11800320 | tf_op jit(solution)/shard_map/reduce_sum | solution.py:95
  213.6 8.1 %fusion.52 = bf16[960,64]{0,1:T(8,128)(2,1)S(1)} fusion(bf16[6144,64]{0,1:T(8,128)(2,1)S(1)} %copy-done, bf16[960,6144]{1,0:T(8,128)(2,1)} %all-gather.5.cloned.1.call-done, f32[6144]{0:T(1024)S(1)} %convert_element_type.144, f32[960]{0:T(1024)S(1)} %add_rsqrt_fusion), kind=kOutput, calls=%fused_computation.53 | convolution fusion | flops 772792320 | bytes 12734208 | tf_op jit(solution)/shard_map/dot_general | solution.py:97
  222.9 6.3 %fusion.23 = f32[960,384]{1,0:T(8,128)S(1)} fusion(bf16[6144,384]{1,0:T(8,128)(2,1)S(1)} %bitcast.96, bf16[960,6144]{1,0:T(8,128)(2,1)S(1)} %copy-done.2, f32[6144]{0:T(1024)S(1)} %convert_element_type.144, f32[960]{0:T(1024)S(1)} %add_rsqrt_fusion), kind=kOutput, calls=%fused_computation.33 | convolution fusion | flops 4547911680 | bytes 18018048 | tf_op jit(solution)/shard_map/dot_general | solution.py:96
  231.1 8.2 %fusion.46 = bf16[960,64]{0,1:T(8,128)(2,1)S(1)} fusion(bf16[6144,64]{0,1:T(8,128)(2,1)} %param.25, bf16[960,6144]{1,0:T(8,128)(2,1)} %all-gather.5.cloned.1.call-done, f32[6144]{0:T(1024)S(1)} %convert_element_type.144, f32[960]{0:T(1024)S(1)} %add_rsqrt_fusion), kind=kOutput, calls=%fused_computation.51 | convolution fusion | flops 772792320 | bytes 12734208 | tf_op jit(solution)/shard_map/dot_general | solution.py:98
  249.6 12.0 %convolution_convert_fusion = bf16[960,6144]{1,0:T(8,128)(2,1)} fusion(bf16[384,6144]{1,0:T(8,128)(2,1)} %param.26, bf16[480,384]{0,1:T(8,128)(2,1)S(1)} %bitcast.91, bf16[480,384]{0,1:T(8,128)(2,1)S(1)} %bitcast.90), kind=kOutput, calls=%fused_computation.16 | convolution fusion | flops 4537221120 | bytes 17252352 | tf_op jit(solution)/shard_map/dot_general | solution.py:127
  261.6 16.4 %copy.83 = bf16[960,6144]{0,1:T(8,128)(2,1)} copy(bf16[960,6144]{1,0:T(8,128)(2,1)} %convolution_convert_fusion) | data formatting | bytes 23592960
  278.7 94.9 %reduce-scatter.4.cloned.1.call-done = bf16[384,960]{1,0:T(8,128)(2,1)} async-done(((bf16[6144,960]{1,0:T(8,128)(2,1)}), bf16[384,960]{1,0:T(8,128)(2,1)}) %reduce-scatter.4.cloned.1.call-update) | async-done | bytes 737296
  376.1 15.8 %all_gather.11 = bf16[2,6144]{1,0:T(2,128)(2,1)S(1)} all-gather(bf16[2,384]{1,0:T(2,128)(2,1)S(1)} %gather_fusion.1), channel_id=1, replica_groups=mesh['req'=8,'hid'=16] {'hid'}, dimensions={1}, use_global_device_ids=true | all-gather | bytes 26112 | tf_op jit(solution)/shard_map/all_gather | solution.py:137
  391.8 8.5 %collective-permute-start.2 = (bf16[2,6144]{1,0:T(2,128)(2,1)S(1)}, bf16[2,6144]{1,0:T(2,128)(2,1)S(1)}, u32[]{:S(2)}, u32[]{:S(2)}) collective-permute-start(bf16[2,6144]{1,0:T(2,128)(2,1)S(1)} %all_gather.11), channel_id=1, source_target_pairs={{0,16},{16,32},{32,48},{48,64},{64,80},{80,96},{96,112},{112,0},{1... | collective-permute-start | bytes 73736 | tf_op jit(solution)/shard_map/ppermute | solution.py:140
  401.3 2.3 collective-permute-start.3
  404.5 2.3 collective-permute-start.4
  406.9 2.0 collective-permute-done.4
  410.1 3.2 collective-permute-done.5
  413.4 4.4 collective-permute-done.6
  417.8 4.5 collective-permute-done.7
  422.3 4.4 collective-permute-done.8
  428.0 3.8 convolution_reduce_fusion
  431.8 65.5 %pmax.7 = f32[16]{0:T(128)} all-reduce(f32[16]{0:T(128)S(1)} %convolution_reduce_fusion), channel_id=1, replica_groups=mesh['req'=8,'hid'=16] {'req','hid'}, use_global_device_ids=true, to_apply=%region_11.12 | all-reduce | flops 16 | bytes 128 | tf_op jit(solution)/shard_map/pmax | solution.py:153
  (119 shorter events, 35.2 us)
Async XLA Ops:
  7.2 206.5 %copy-start = (bf16[6144,64]{0,1:T(8,128)(2,1)S(1)}, bf16[6144,64]{0,1:T(8,128)(2,1)}, u32[]{:S(2)}) copy-start(bf16[6144,64]{0,1:T(8,128)(2,1)} %param.24) | copy-start | bytes 2359300
  7.2 28.0 %copy-start.13 = (bf16[12800]{0:T(1024)(128)(2,1)S(1)}, bf16[12800]{0:T(1024)(128)(2,1)}, u32[]{:S(2)}) copy-start(bf16[12800]{0:T(1024)(128)(2,1)} %param.18) | copy-start | bytes 76804
  7.2 82.2 %all-gather.3.cloned.1.call-start = ((), (), s32[]{:S(2)}) async-start(), calls=%async_computation.2 | async-start | bytes 6963200 | tf_op jit(solution)/shard_map/all_gather | solution.py:74
  10.6 83.7 %copy-start.20 = (f32[384]{0:T(512)S(1)}, f32[384]{0:T(512)}, u32[]{:S(2)}) copy-start(f32[384]{0:T(512)} %param.20) | copy-start | bytes 4612
  26.1 180.7 %all-gather.5.cloned.1.call-start = ((), (), s32[]{:S(2)}) async-start(), calls=%async_computation.3 | async-start | bytes 12533760 | tf_op jit(solution)/shard_map/all_gather | solution.py:93
  94.3 15.6 %copy-start.5 = (bf16[2,480,384]{2,1,0:T(8,128)(2,1)S(1)}, bf16[2,480,384]{2,1,0:T(8,128)(2,1)}, u32[]{:S(2)}) copy-start(bf16[2,480,384]{2,1,0:T(8,128)(2,1)} %param.21) | copy-start | bytes 2211844
  94.3 18.0 %copy-start.14 = (bf16[6144]{0:T(1024)(128)(2,1)S(1)}, bf16[6144]{0:T(1024)(128)(2,1)}, u32[]{:S(2)}) copy-start(bf16[6144]{0:T(1024)(128)(2,1)} %param.22) | copy-start | bytes 36868
  94.3 18.0 %copy-start.16 = (s32[2]{0:T(128)S(1)}, s32[2]{0:T(128)}, u32[]{:S(2)}) copy-start(s32[2]{0:T(128)} %param.29) | copy-start | bytes 28
  112.2 261.4 %reduce-scatter.4.cloned.1.call-start = ((), (), s32[]{:S(2)}) async-start(), calls=%async_computation.4 | async-start | bytes 13369344
  112.3 101.3 %copy-start.18 = (f32[64]{0:T(128)}, f32[64]{0:T(128)S(1)}, u32[]{:S(2)}) copy-start(f32[64]{0:T(128)S(1)} %multiply_exponential_fusion) | copy-start | bytes 772
  206.8 16.1 %slice-start = ((s8[4718592]{0:T(1024)(128)(4,1)}), s8[524288]{0:T(1024)(128)(4,1)S(1)}, s32[]{:S(2)}) async-start(s8[4718592]{0:T(1024)(128)(4,1)} %bitcast.95), calls=%async_computation.5 | async-start | bytes 1048576
  221.8 19.5 %collective-permute-start.1 = (bf16[960,64]{0,1:T(8,128)(2,1)S(1)}, bf16[960,64]{0,1:T(8,128)(2,1)}, u32[]{:S(2)}, u32[]{:S(2)}) collective-permute-start(bf16[960,64]{0,1:T(8,128)(2,1)S(1)} %fusion.52), channel_id=1, source_target_pairs={{0,1},{1,0},{2,3},{3,2},{4,5},{5,4},{6,7},{7,6},{8,9},{9,8},{10,11... | collective-permute-start | bytes 368648 | tf_op jit(solution)/shard_map/ppermute | solution.py:19
  239.2 6.0 %collective-permute-start = (bf16[960,64]{0,1:T(8,128)(2,1)S(1)}, bf16[960,64]{0,1:T(8,128)(2,1)S(1)}, u32[]{:S(2)}, u32[]{:S(2)}) collective-permute-start(bf16[960,64]{0,1:T(8,128)(2,1)S(1)} %fusion.46), channel_id=1, source_target_pairs={{0,1},{1,0},{2,3},{3,2},{4,5},{5,4},{6,7},{7,6},{8,9},{9,8},{10,11... | collective-permute-start | bytes 368648 | tf_op jit(solution)/shard_map/ppermute | solution.py:19
  278.0 97.1 %copy-start.4 = (bf16[2,480,384]{2,1,0:T(8,128)(2,1)S(1)}, bf16[2,480,384]{2,1,0:T(8,128)(2,1)}, u32[]{:S(2)}) copy-start(bf16[2,480,384]{2,1,0:T(8,128)(2,1)} %copy-done.3) | copy-start | bytes 2211844
  278.0 144.2 %copy-start.15 = (bf16[6144]{0:T(1024)(128)(2,1)S(1)}, bf16[6144]{0:T(1024)(128)(2,1)}, u32[]{:S(2)}) copy-start(bf16[6144]{0:T(1024)(128)(2,1)} %param.27) | copy-start | bytes 36868
  373.6 123.7 %copy-start.1 = (bf16[6144,64]{0,1:T(8,128)(2,1)S(1)}, bf16[6144,64]{0,1:T(8,128)(2,1)}, u32[]{:S(2)}) copy-start(bf16[6144,64]{0,1:T(8,128)(2,1)} %param.24) | copy-start | bytes 2359300
  375.4 121.9 %copy-start.10 = (bf16[960,384]{1,0:T(8,128)(2,1)}, bf16[960,384]{1,0:T(8,128)(2,1)S(1)}, u32[]{:S(2)}) copy-start(bf16[960,384]{1,0:T(8,128)(2,1)S(1)} %add_convert_fusion) | copy-start | bytes 2211844
  391.8 9.5 %collective-permute-start.2 = (bf16[2,6144]{1,0:T(2,128)(2,1)S(1)}, bf16[2,6144]{1,0:T(2,128)(2,1)S(1)}, u32[]{:S(2)}, u32[]{:S(2)}) collective-permute-start(bf16[2,6144]{1,0:T(2,128)(2,1)S(1)} %all_gather.11), channel_id=1, source_target_pairs={{0,16},{16,32},{32,48},{48,64},{64,80},{80,96},{96,112},{112,0},{1... | collective-permute-start | bytes 73736 | tf_op jit(solution)/shard_map/ppermute | solution.py:140
  401.3 3.3 collective-permute-start.3
  404.5 4.3 collective-permute-start.4
  408.9 4.5 collective-permute-start.5
  413.3 4.5 collective-permute-start.6
  417.8 4.5 collective-permute-start.7
  422.2 4.5 collective-permute-start.8
  (13 other events, 56.4 us)
Sparse Core Ops, SparseCore 0:
  26.2 63.1 all-gather.2
  112.3 94.4 all-gather.4
  278.2 95.3 reduce-scatter.3
